TPU v7x, 512 devices: a whole 4x8x8 slice. The times are simulated.
512 devices in a mesh: row: 16 (over z, y_lo), col: 32 (over x, y_hi, core).
Axes of the slice: x: 4, y: 8 (y_hi: 4, y_lo: 2; y = y_hi * 2 + y_lo), z: 8, core: 2. Of those that a mesh axis runs over, the one named last changes fastest.
Arguments:
- green_blocks: bfloat16 [16, 32, 12, 2, 288, 288], P('row', 'col'), may hold values from -0.0625 to 0.0625
- slot_rows: int32 [16, 32, 12], P('row', 'col'), may hold values from 0 to 7, as said below
- slot_cols: int32 [16, 32, 12], P('row', 'col'), may hold values from 0 to 3
- slot_count: int32 [16, 32], P('row', 'col'), may hold values from 2 to 12, as said below
- cell_class: int32 [4, 32, 96], P(None, 'col'), may hold values from 0 to 15
- class_contrast: float32 [16, 2], replicated, may hold values from -0.6 to 0.6
- background: float32 [2, 32, 4, 32, 288], P(None, None, None, 'col'), may hold values from -6 to 6
Outputs:
- total_field: float32 [2, 32, 4, 32, 288], P(None, None, None, 'col')
Inputs may be any that keep to these rules, and one draw needn't show every extreme that they name: slot_rows[r, c, s] and slot_cols[r, c, s] name different block pairs within one device's slots, and every slot, used or not, names a block in the upper triangle: (slot_rows // 2) * 32 + 2 r + slot_rows % 2 is at most slot_cols * 32 + c. Slots from slot_count[r, c] on are not used. `slot_count`: some device holds exactly 12 stored blocks.
All inputs are finite; a program needn't handle non-finite values.
Results may differ from a plain program's by a relative error of at most 0.0033.
Values may be sent and summed in bfloat16 or wider, within the bound.
A program may use at most 64 MiB of HBM per device.

v0:
```python
import jax
import jax.numpy as jnp
from jax import lax
from jax.sharding import PartitionSpec as P

PRODUCTS = 3


def from_root(array, axis, root):
    mine = lax.axis_index(axis) == root
    return lax.psum(jnp.where(mine, array, jnp.zeros_like(array)), axis)


def complex_scale(field_now, contrast_re, contrast_im):
    real_part = field_now[0]
    imag_part = field_now[1]
    scaled = jnp.stack(
        [
            contrast_re * real_part - contrast_im * imag_part,
            contrast_re * imag_part + contrast_im * real_part,
        ]
    )
    return scaled.astype(jnp.bfloat16)


def combine(products):
    return jnp.stack([products[0, 0] - products[1, 1], products[0, 1] + products[1, 0]])


def local(green_blocks, slot_rows, slot_cols, slot_count, cell_class, class_contrast, background):
    row_index = lax.axis_index("row")
    col_index = lax.axis_index("col")
    stride = lax.axis_size("col")
    green_tiles = green_blocks[0, 0]
    slot_total = green_tiles.shape[0]
    entries = green_tiles.shape[-1]
    sources = background.shape[1]
    col_blocks = background.shape[2]
    row_blocks = 2 * col_blocks
    local_rows = slot_rows[0, 0]
    local_cols = slot_cols[0, 0]
    global_rows = local_rows // 2 * stride + 2 * row_index + local_rows % 2
    global_cols = local_cols * stride + col_index
    off_diagonal = (global_rows != global_cols).astype(jnp.float32)
    living = (jnp.arange(slot_total) < slot_count[0, 0]).astype(jnp.float32)
    row_pick = (local_rows[:, None] == jnp.arange(row_blocks)[None, :]).astype(
        jnp.float32
    ) * living[:, None]
    col_pick = (local_cols[:, None] == jnp.arange(col_blocks)[None, :]).astype(jnp.float32) * (
        living * off_diagonal
    )[:, None]
    classes = class_contrast.shape[0]
    lookup = (cell_class[:, 0, :, None] == jnp.arange(classes)[None, None, :]).astype(jnp.float32)
    values = jnp.einsum("bte,ec->btc", lookup, class_contrast, precision=lax.Precision.HIGHEST)
    contrast_re = jnp.tile(values[:, :, 0], (1, 3))
    contrast_im = jnp.tile(values[:, :, 1], (1, 3))
    start_field = background[:, :, :, 0, :]
    field_now = start_field
    current = complex_scale(field_now, contrast_re, contrast_im)
    for step_index in range(PRODUCTS):
        final_step = step_index + 1 == PRODUCTS
        halves = [from_root(current, "col", 2 * row_index + parity) for parity in range(2)]
        row_current = jnp.stack(halves, axis=3).reshape(2, sources, row_blocks, entries)
        direct_in = jnp.take(current, local_cols, axis=2)
        mirror_in = jnp.take(row_current, local_rows, axis=2)
        direct_terms = combine(
            jnp.einsum(
                "sqoi,pksi->qpkso", green_tiles, direct_in, preferred_element_type=jnp.float32
            )
        )
        mirror_terms = combine(
            jnp.einsum(
                "sqoi,pkso->qpksi", green_tiles, mirror_in, preferred_element_type=jnp.float32
            )
        )
        direct_part = jnp.einsum(
            "pkse,sb->pkbe", direct_terms, row_pick, precision=lax.Precision.HIGHEST
        )
        mirror_part = jnp.einsum(
            "pkse,sb->pkbe", mirror_terms, col_pick, precision=lax.Precision.HIGHEST
        )
        row_total = lax.psum(direct_part, "col")
        owned_part = lax.dynamic_index_in_dim(
            row_total.reshape(2, sources, col_blocks, 2, entries),
            col_index % 2,
            axis=3,
            keepdims=False,
        )
        direct_here = from_root(owned_part, "row", col_index // 2)
        column_total = lax.psum(mirror_part, "row")
        field_now = start_field + column_total + direct_here
        if not final_step:
            current = complex_scale(field_now, contrast_re, contrast_im)
    return field_now[:, :, :, None, :]


def solution(mesh):
    in_specs = (
        P("row", "col", None, None, None, None),
        P("row", "col", None),
        P("row", "col", None),
        P("row", "col"),
        P(None, "col", None),
        P(),
        P(None, None, None, "col", None),
    )
    out_specs = P(None, None, None, "col", None)
    return jax.shard_map(local, mesh=mesh, in_specs=in_specs, out_specs=out_specs, check_vma=False)
```

profile of v0, /device:TPU:2, one launch (start us, length us, event | category | flops | bytes accessed | tf_op | source)
XLA Modules:
  0.0 2183.8 jit_solution(12541447128961993889)
XLA Ops:
  6.6 0.7 copy-done
  7.2 0.8 fusion.106
  8.0 0.1 tile.20
  8.1 0.1 tile.23
  8.2 1.3 fusion.152
  9.5 0.1 subtract_convert_fusion.2
  9.6 1.0 select_bitcast_fusion.8
  10.8 0.7 gather_fusion.1
  11.5 4.6 fusion.15
  16.1 0.1 fusion.72
  16.9 0.1 pad_maximum_fusion.1
  17.0 1.5 fusion.42
  18.6 0.2 copy.42
  18.8 1.5 copy.43
  20.4 263.5 %all-reduce.32.cloned.1.call-done = (bf16[2,32,4,1,288]{4,2,1,0,3:T(4,128)(2,1)}, bf16[2,32,4,1,288]{4,2,1,0,3:T(4,128)(2,1)}) async-done(((bf16[2,32,4,1,288]{4,2,1,0,3:T(4,128)(2,1)}, bf16[2,32,4,1,288]{4,2,1,0,3:T(4,128)(2,1)}), (bf16[2,32,4,1,288]{4,2,1,0,3:T(4,128)(2,1)}, bf16[2,32,4,1,288]{4,2,1,0,3:T(4,128)(2,1)})) %all-reduce.32.cloned.1.call-update) | async-done | bytes 294928 | tf_op jit(solution)/shard_map/psum | solution.py:11
  283.9 1.3 pad_maximum_fusion.6
  285.3 0.7 gather_fusion
  286.0 3.8 fusion.12
  289.9 0.1 pad_maximum_fusion
  290.0 2.3 fusion.51
  292.4 278.5 %all-reduce.16.cloned.1.call-done = f32[2,32,4,2,288]{4,2,1,0,3:T(4,128)} async-done(((f32[2,32,4,2,288]{4,2,1,0,3:T(4,128)}), f32[2,32,4,2,288]{4,2,1,0,3:T(4,128)}) %all-reduce.16.cloned.1.call-update) | async-done | bytes 589840 | tf_op jit(solution)/shard_map/psum | solution.py:82
  570.9 1.8 select_bitcast_fusion.2
  572.8 157.6 %all-reduce.26.cloned.1.call-done = (f32[2,32,4,288]{3,2,1,0:T(4,128)}, f32[2,32,4,288]{3,2,1,0:T(4,128)}) async-done(((f32[2,32,4,288]{3,2,1,0:T(4,128)}, f32[2,32,4,288]{3,2,1,0:T(4,128)}), (f32[2,32,4,288]{3,2,1,0:T(4,128)}, f32[2,32,4,288]{3,2,1,0:T(4,128)})) %all-reduce.26.cloned.1.call-update) | async-done | bytes 589840 | tf_op jit(solution)/shard_map/psum | solution.py:11
  730.4 1.3 fusion.96
  731.7 0.1 subtract_convert_fusion.1
  731.8 1.0 select_bitcast_fusion.6
  732.9 0.7 gather_fusion.3
  733.6 4.6 fusion.21
  738.4 0.2 all-reduce.18.cloned.1.call-start
  738.6 0.1 pad_maximum_fusion.3
  738.7 1.5 fusion.45
  740.2 0.2 copy.52
  740.4 1.5 copy.53
  741.9 264.5 %all-reduce.30.cloned.1.call-done = (bf16[2,32,4,1,288]{4,2,1,0,3:T(4,128)(2,1)}, bf16[2,32,4,1,288]{4,2,1,0,3:T(4,128)(2,1)}) async-done(((bf16[2,32,4,1,288]{4,2,1,0,3:T(4,128)(2,1)}, bf16[2,32,4,1,288]{4,2,1,0,3:T(4,128)(2,1)}), (bf16[2,32,4,1,288]{4,2,1,0,3:T(4,128)(2,1)}, bf16[2,32,4,1,288]{4,2,1,0,3:T(4,128)(2,1)})) %all-reduce.30.cloned.1.call-update) | async-done | bytes 294928 | tf_op jit(solution)/shard_map/psum | solution.py:11
  1006.4 1.3 pad_maximum_fusion.7
  1007.8 0.7 gather_fusion.2
  1008.4 3.8 fusion.18
  1012.4 0.1 pad_maximum_fusion.2
  1012.5 2.3 fusion.54
  1014.8 278.1 %all-reduce.18.cloned.1.call-done = f32[2,32,4,2,288]{4,2,1,0,3:T(4,128)} async-done(((f32[2,32,4,2,288]{4,2,1,0,3:T(4,128)}), f32[2,32,4,2,288]{4,2,1,0,3:T(4,128)}) %all-reduce.18.cloned.1.call-update) | async-done | bytes 589840 | tf_op jit(solution)/shard_map/psum | solution.py:82
  1292.9 1.8 select_bitcast_fusion.1
  1294.8 157.7 %all-reduce.24.cloned.1.call-done = (f32[2,32,4,288]{3,2,1,0:T(4,128)}, f32[2,32,4,288]{3,2,1,0:T(4,128)}) async-done(((f32[2,32,4,288]{3,2,1,0:T(4,128)}, f32[2,32,4,288]{3,2,1,0:T(4,128)}), (f32[2,32,4,288]{3,2,1,0:T(4,128)}, f32[2,32,4,288]{3,2,1,0:T(4,128)})) %all-reduce.24.cloned.1.call-update) | async-done | bytes 589840 | tf_op jit(solution)/shard_map/psum | solution.py:11
  1452.5 1.3 fusion.97
  1453.8 0.1 subtract_convert_fusion
  1453.9 1.0 select_bitcast_fusion.4
  1455.0 0.7 gather_fusion.5
  1455.6 4.6 fusion.27
  1460.3 0.1 fusion.62
  1460.5 0.1 pad_maximum_fusion.5
  1460.6 1.5 fusion.48
  1462.1 0.2 copy.62
  1462.3 1.5 copy.63
  1463.8 0.3 all-reduce.22.cloned.1.call-start
  1464.1 264.4 %all-reduce.28.cloned.1.call-done = (bf16[2,32,4,1,288]{4,2,1,0,3:T(4,128)(2,1)}, bf16[2,32,4,1,288]{4,2,1,0,3:T(4,128)(2,1)}) async-done(((bf16[2,32,4,1,288]{4,2,1,0,3:T(4,128)(2,1)}, bf16[2,32,4,1,288]{4,2,1,0,3:T(4,128)(2,1)}), (bf16[2,32,4,1,288]{4,2,1,0,3:T(4,128)(2,1)}, bf16[2,32,4,1,288]{4,2,1,0,3:T(4,128)(2,1)})) %all-reduce.28.cloned.1.call-update) | async-done | bytes 294928 | tf_op jit(solution)/shard_map/psum | solution.py:11
  1728.5 1.3 pad_maximum_fusion.8
  1729.8 0.7 gather_fusion.4
  1730.5 3.8 fusion.24
  1734.5 0.1 pad_maximum_fusion.4
  1734.6 2.3 fusion.57
  1736.9 278.5 %all-reduce.20.cloned.1.call-done = f32[2,32,4,2,288]{4,2,1,0,3:T(4,128)} async-done(((f32[2,32,4,2,288]{4,2,1,0,3:T(4,128)}), f32[2,32,4,2,288]{4,2,1,0,3:T(4,128)}) %all-reduce.20.cloned.1.call-update) | async-done | bytes 589840 | tf_op jit(solution)/shard_map/psum | solution.py:82
  2015.4 1.8 select_bitcast_fusion
  2017.3 157.5 %all-reduce.22.cloned.1.call-done = (f32[2,32,4,288]{3,2,1,0:T(4,128)}, f32[2,32,4,288]{3,2,1,0:T(4,128)}) async-done(((f32[2,32,4,288]{3,2,1,0:T(4,128)}, f32[2,32,4,288]{3,2,1,0:T(4,128)}), (f32[2,32,4,288]{3,2,1,0:T(4,128)}, f32[2,32,4,288]{3,2,1,0:T(4,128)})) %all-reduce.22.cloned.1.call-update) | async-done | bytes 589840 | tf_op jit(solution)/shard_map/psum | solution.py:11
  2174.8 1.3 fusion.99
  2176.1 1.1 copy.64
  (48 shorter events, 1.4 us)
Async XLA Ops:
  6.5 0.7 copy-start
  6.5 4.2 copy-start.3
  6.5 4.2 copy-start.2
  6.5 277.4 %all-reduce.32.cloned.1.call-start = ((), (), s32[]{:S(2)}) async-start(), calls=%async_computation.8 | async-start | bytes 786432 | tf_op jit(solution)/shard_map/psum | solution.py:11
  10.7 560.2 %all-reduce.16.cloned.1.call-start = ((), (), s32[]{:S(2)}) async-start(), calls=%async_computation | async-start | bytes 1572864 | tf_op jit(solution)/shard_map/psum | solution.py:82
  20.2 710.1 %all-reduce.26.cloned.1.call-start = ((), (), s32[]{:S(2)}) async-start(), calls=%async_computation.5 | async-start | bytes 1572864 | tf_op jit(solution)/shard_map/psum | solution.py:11
  290.0 440.4 %copy-start.1 = (f32[2,32,4,1,288]{4,3,2,1,0:T(1,128)S(1)}, f32[2,32,4,1,288]{4,3,2,1,0:T(1,128)}, u32[]{:S(2)}) copy-start(f32[2,32,4,1,288]{4,3,2,1,0:T(1,128)} %param.17) | copy-start | bytes 884740
  572.7 433.6 %all-reduce.30.cloned.1.call-start = ((), (), s32[]{:S(2)}) async-start(), calls=%async_computation.7 | async-start | bytes 786432 | tf_op jit(solution)/shard_map/psum | solution.py:11
  738.4 554.6 %all-reduce.18.cloned.1.call-start = ((), (), s32[]{:S(2)}) async-start(), calls=%async_computation.1 | async-start | bytes 1572864 | tf_op jit(solution)/shard_map/psum | solution.py:82
  741.9 710.6 %all-reduce.24.cloned.1.call-start = ((), (), s32[]{:S(2)}) async-start(), calls=%async_computation.4 | async-start | bytes 1572864 | tf_op jit(solution)/shard_map/psum | solution.py:11
  1294.8 433.7 %all-reduce.28.cloned.1.call-start = ((), (), s32[]{:S(2)}) async-start(), calls=%async_computation.6 | async-start | bytes 786432 | tf_op jit(solution)/shard_map/psum | solution.py:11
  1460.5 555.0 %all-reduce.20.cloned.1.call-start = ((), (), s32[]{:S(2)}) async-start(), calls=%async_computation.2 | async-start | bytes 1572864 | tf_op jit(solution)/shard_map/psum | solution.py:82
  1463.8 711.0 %all-reduce.22.cloned.1.call-start = ((), (), s32[]{:S(2)}) async-start(), calls=%async_computation.3 | async-start | bytes 1572864 | tf_op jit(solution)/shard_map/psum | solution.py:11
Sparse Core Ops, SparseCore 0:
  10.8 273.0 all-reduce.31
  287.1 283.7 all-reduce.15
  573.8 156.5 all-reduce.25
  738.5 267.8 all-reduce.29
  1009.1 283.7 all-reduce.17
  1296.0 156.4 all-reduce.23
  1460.6 267.8 all-reduce.27
  1731.6 283.7 all-reduce.19
  2018.4 156.3 all-reduce.21
where the time goes:
time: 2180 us
  waiting for transfers between devices  2100 us (96%)
  matrix products  37.7 us (2%)
    psum x6, waiting for transfers between devices, from_root(): return lax.psum(jnp.where(mine, array, jnp.zeros_like(array)), axis)  1270 us
    psum x3, waiting for transfers between devices, local(): row_total = lax.psum(direct_part, 'col')  835 us
  transfers between devices with their start and end apart: 9, of which 9 were waited for; matrix products, arithmetic and copies ran while one was open for 2% of the time, Pallas kernels for 0%

commit v1 on v0

--- a/solution.py
+++ b/solution.py
@@ -79,7 +79,7 @@
         mirror_part = jnp.einsum(
             "pkse,sb->pkbe", mirror_terms, col_pick, precision=lax.Precision.HIGHEST
         )
-        row_total = lax.psum(direct_part, "col")
+        row_total = jnp.sum(lax.all_gather(direct_part, "col"), axis=0)
         owned_part = lax.dynamic_index_in_dim(
             row_total.reshape(2, sources, col_blocks, 2, entries),
             col_index % 2,

time: 2180 us -> 1840 us (0.84)
  waiting for transfers between devices: 2100 us -> 1730 us
  other arithmetic: 18.1 us -> 44 us
    psum x3 -> x0, waiting for transfers between devices: 835 us -> none  [local(): row_total = lax.psum(direct_part, 'col')]
    all_gather x0 -> x3, waiting for transfers between devices: none -> 506 us  [local(): row_total = jnp.sum(lax.all_gather(direct_part, 'col'), axis=0)]
    psum x6, waiting for transfers between devices: 1270 us -> 1220 us  [from_root(): return lax.psum(jnp.where(mine, array, jnp.zeros_like(array)), axis)]
    reduce_sum x0 -> x3, other arithmetic: none -> 28.2 us  [local(): row_total = jnp.sum(lax.all_gather(direct_part, 'col'), axis=0)]
where the time goes in v1:
time: 1840 us
  waiting for transfers between devices  1730 us (94%)
  other arithmetic  44 us (2%)
  matrix products  40.5 us (2%)
    psum x6, waiting for transfers between devices, from_root(): return lax.psum(jnp.where(mine, array, jnp.zeros_like(array)), axis)  1220 us
    all_gather x3, waiting for transfers between devices, local(): row_total = jnp.sum(lax.all_gather(direct_part, 'col'), axis=0)  506 us
  transfers between devices with their start and end apart: 9, of which 9 were waited for; matrix products, arithmetic and copies ran while one was open for 2% of the time, Pallas kernels for 0%

profile of v1, /device:TPU:2, one launch (start us, length us, event | category | flops | bytes accessed | tf_op | source)
XLA Modules:
  0.0 1837.7 jit_solution(7577803729780252532)
XLA Ops:
  6.5 1.3 fusion.155
  7.9 0.8 fusion.109
  8.7 0.1 tile.23
  8.8 0.1 tile.20
  8.9 0.1 subtract_convert_fusion.2
  9.0 1.0 select_bitcast_fusion.5
  10.2 0.7 gather_fusion.1
  10.9 4.6 fusion.15
  15.5 0.1 fusion.72
  15.6 0.1 fusion.74
  16.3 0.1 pad_maximum_fusion.1
  16.4 2.5 fusion.42
  19.1 264.4 %all-reduce.23.cloned.1.call-done = (bf16[2,32,4,1,288]{4,2,1,0,3:T(4,128)(2,1)}, bf16[2,32,4,1,288]{4,2,1,0,3:T(4,128)(2,1)}) async-done(((bf16[2,32,4,1,288]{4,2,1,0,3:T(4,128)(2,1)}, bf16[2,32,4,1,288]{4,2,1,0,3:T(4,128)(2,1)}), (bf16[2,32,4,1,288]{4,2,1,0,3:T(4,128)(2,1)}, bf16[2,32,4,1,288]{4,2,1,0,3:T(4,128)(2,1)})) %all-reduce.23.cloned.1.call-update) | async-done | bytes 294928 | tf_op jit(solution)/shard_map/psum | solution.py:11
  283.5 1.3 pad_maximum_fusion.6
  284.8 0.7 gather_fusion
  285.5 3.8 fusion.12
  289.4 0.1 fusion.77
  289.5 0.1 pad_maximum_fusion
  289.6 2.3 fusion.51
  291.9 168.7 %all-gather.7.cloned.1.call-done = f32[64,32,8,288]{3,2,1,0:T(8,128)} async-done(((f32[2,32,8,288]{3,2,1,0:T(8,128)}), f32[64,32,8,288]{3,2,1,0:T(8,128)}) %all-gather.7.cloned.1.call-update) | async-done | bytes 18874384 | tf_op jit(solution)/shard_map/all_gather | solution.py:82
  460.5 9.4 reduce_sum.27
  470.0 0.2 copy.72
  470.2 1.0 fusion.98
  471.3 143.3 %all-reduce.17.cloned.1.call-done = (f32[2,32,4,288]{3,2,1,0:T(4,128)}, f32[2,32,4,288]{3,2,1,0:T(4,128)}) async-done(((f32[2,32,4,288]{3,2,1,0:T(4,128)}, f32[2,32,4,288]{3,2,1,0:T(4,128)}), (f32[2,32,4,288]{3,2,1,0:T(4,128)}, f32[2,32,4,288]{3,2,1,0:T(4,128)})) %all-reduce.17.cloned.1.call-update) | async-done | bytes 589840 | tf_op jit(solution)/shard_map/psum | solution.py:11
  614.6 1.3 fusion.99
  615.9 0.1 subtract_convert_fusion.1
  616.0 1.0 select_bitcast_fusion.3
  617.1 0.7 gather_fusion.3
  617.8 4.6 fusion.21
  622.6 0.2 all-gather.9.cloned.1.call-start
  622.8 0.1 pad_maximum_fusion.3
  622.9 2.5 fusion.45
  625.5 265.1 %all-reduce.21.cloned.1.call-done = (bf16[2,32,4,1,288]{4,2,1,0,3:T(4,128)(2,1)}, bf16[2,32,4,1,288]{4,2,1,0,3:T(4,128)(2,1)}) async-done(((bf16[2,32,4,1,288]{4,2,1,0,3:T(4,128)(2,1)}, bf16[2,32,4,1,288]{4,2,1,0,3:T(4,128)(2,1)}), (bf16[2,32,4,1,288]{4,2,1,0,3:T(4,128)(2,1)}, bf16[2,32,4,1,288]{4,2,1,0,3:T(4,128)(2,1)})) %all-reduce.21.cloned.1.call-update) | async-done | bytes 294928 | tf_op jit(solution)/shard_map/psum | solution.py:11
  890.6 1.3 pad_maximum_fusion.7
  892.0 0.7 gather_fusion.2
  892.7 3.8 fusion.18
  896.6 0.1 pad_maximum_fusion.2
  896.7 2.3 fusion.54
  899.0 168.5 %all-gather.9.cloned.1.call-done = f32[64,32,8,288]{3,2,1,0:T(8,128)} async-done(((f32[2,32,8,288]{3,2,1,0:T(8,128)}), f32[64,32,8,288]{3,2,1,0:T(8,128)}) %all-gather.9.cloned.1.call-update) | async-done | bytes 18874384 | tf_op jit(solution)/shard_map/all_gather | solution.py:82
  1067.5 9.4 reduce_sum.28
  1076.9 0.2 copy.82
  1077.2 1.0 fusion.97
  1078.3 143.3 %all-reduce.15.cloned.1.call-done = (f32[2,32,4,288]{3,2,1,0:T(4,128)}, f32[2,32,4,288]{3,2,1,0:T(4,128)}) async-done(((f32[2,32,4,288]{3,2,1,0:T(4,128)}, f32[2,32,4,288]{3,2,1,0:T(4,128)}), (f32[2,32,4,288]{3,2,1,0:T(4,128)}, f32[2,32,4,288]{3,2,1,0:T(4,128)})) %all-reduce.15.cloned.1.call-update) | async-done | bytes 589840 | tf_op jit(solution)/shard_map/psum | solution.py:11
  1221.6 1.3 fusion.100
  1222.9 0.1 subtract_convert_fusion
  1223.0 1.0 select_bitcast_fusion.1
  1224.1 0.7 gather_fusion.5
  1224.7 4.6 fusion.27
  1229.6 0.1 pad_maximum_fusion.5
  1229.7 2.5 fusion.48
  1232.2 0.3 all-reduce.13.cloned.1.call-start
  1232.5 265.1 %all-reduce.19.cloned.1.call-done = (bf16[2,32,4,1,288]{4,2,1,0,3:T(4,128)(2,1)}, bf16[2,32,4,1,288]{4,2,1,0,3:T(4,128)(2,1)}) async-done(((bf16[2,32,4,1,288]{4,2,1,0,3:T(4,128)(2,1)}, bf16[2,32,4,1,288]{4,2,1,0,3:T(4,128)(2,1)}), (bf16[2,32,4,1,288]{4,2,1,0,3:T(4,128)(2,1)}, bf16[2,32,4,1,288]{4,2,1,0,3:T(4,128)(2,1)})) %all-reduce.19.cloned.1.call-update) | async-done | bytes 294928 | tf_op jit(solution)/shard_map/psum | solution.py:11
  1497.6 1.3 pad_maximum_fusion.8
  1498.9 0.7 gather_fusion.4
  1499.6 3.8 fusion.24
  1503.6 0.1 pad_maximum_fusion.4
  1503.7 2.3 fusion.57
  1506.0 168.7 %all-gather.11.cloned.1.call-done = f32[64,32,8,288]{3,2,1,0:T(8,128)} async-done(((f32[2,32,8,288]{3,2,1,0:T(8,128)}), f32[64,32,8,288]{3,2,1,0:T(8,128)}) %all-gather.11.cloned.1.call-update) | async-done | bytes 18874384 | tf_op jit(solution)/shard_map/all_gather | solution.py:82
  1674.6 9.4 reduce_sum.29
  1684.1 0.2 copy.92
  1684.3 1.0 fusion.96
  1685.3 143.4 %all-reduce.13.cloned.1.call-done = (f32[2,32,4,288]{3,2,1,0:T(4,128)}, f32[2,32,4,288]{3,2,1,0:T(4,128)}) async-done(((f32[2,32,4,288]{3,2,1,0:T(4,128)}, f32[2,32,4,288]{3,2,1,0:T(4,128)}), (f32[2,32,4,288]{3,2,1,0:T(4,128)}, f32[2,32,4,288]{3,2,1,0:T(4,128)})) %all-reduce.13.cloned.1.call-update) | async-done | bytes 589840 | tf_op jit(solution)/shard_map/psum | solution.py:11
  1828.7 1.3 fusion.102
  1830.0 1.1 copy.94
  (55 shorter events, 1.4 us)
Async XLA Ops:
  6.5 1.3 copy-start
  6.5 3.6 copy-start.3
  6.5 276.9 %all-reduce.23.cloned.1.call-start = ((), (), s32[]{:S(2)}) async-start(), calls=%async_computation.8 | async-start | bytes 786432 | tf_op jit(solution)/shard_map/psum | solution.py:11
  10.0 450.5 %all-gather.7.cloned.1.call-start = ((), (), s32[]{:S(2)}) async-start(), calls=%async_computation | async-start | bytes 25952256 | tf_op jit(solution)/shard_map/all_gather | solution.py:82
  15.6 0.8 copy-start.4
  19.0 595.6 %all-reduce.17.cloned.1.call-start = ((), (), s32[]{:S(2)}) async-start(), calls=%async_computation.5 | async-start | bytes 1572864 | tf_op jit(solution)/shard_map/psum | solution.py:11
  470.1 144.5 %copy-start.2 = (f32[2,32,4,1,288]{4,3,2,1,0:T(1,128)S(1)}, f32[2,32,4,1,288]{4,3,2,1,0:T(1,128)}, u32[]{:S(2)}) copy-start(f32[2,32,4,1,288]{4,3,2,1,0:T(1,128)} %param.17) | copy-start | bytes 884740
  471.2 419.3 %all-reduce.21.cloned.1.call-start = ((), (), s32[]{:S(2)}) async-start(), calls=%async_computation.7 | async-start | bytes 786432 | tf_op jit(solution)/shard_map/psum | solution.py:11
  622.6 444.9 %all-gather.9.cloned.1.call-start = ((), (), s32[]{:S(2)}) async-start(), calls=%async_computation.1 | async-start | bytes 25952256 | tf_op jit(solution)/shard_map/all_gather | solution.py:82
  625.4 596.1 %all-reduce.15.cloned.1.call-start = ((), (), s32[]{:S(2)}) async-start(), calls=%async_computation.4 | async-start | bytes 1572864 | tf_op jit(solution)/shard_map/psum | solution.py:11
  1078.2 419.3 %all-reduce.19.cloned.1.call-start = ((), (), s32[]{:S(2)}) async-start(), calls=%async_computation.6 | async-start | bytes 786432 | tf_op jit(solution)/shard_map/psum | solution.py:11
  1229.5 445.1 %all-gather.11.cloned.1.call-start = ((), (), s32[]{:S(2)}) async-start(), calls=%async_computation.2 | async-start | bytes 25952256 | tf_op jit(solution)/shard_map/all_gather | solution.py:82
  1232.2 596.5 %all-reduce.13.cloned.1.call-start = ((), (), s32[]{:S(2)}) async-start(), calls=%async_computation.3 | async-start | bytes 1572864 | tf_op jit(solution)/shard_map/psum | solution.py:11
  1685.3 145.9 %copy-start.1 = (f32[16,2]{0,1:T(2,128)S(1)}, f32[16,2]{0,1:T(2,128)}, u32[]{:S(2)}) copy-start(f32[16,2]{0,1:T(2,128)} %param.16) | copy-start | bytes 388
Sparse Core Ops, SparseCore 0:
  10.3 273.0 all-reduce.22
  287.0 173.4 all-gather.6
  471.4 143.1 all-reduce.16
  622.7 267.8 all-reduce.20
  894.0 173.4 all-gather.8
  1078.3 143.1 all-reduce.14
  1229.7 267.8 all-reduce.18
  1501.1 173.4 all-gather.10
  1685.4 143.1 all-reduce.12
